TPU v7x, 32 devices: a whole 2x2x4 slice. The times are simulated.
32 devices in a mesh: ctx: 8 (over z, x), head: 4 (over y, core).
Axes of the slice: x: 2, y: 2, z: 4, core: 2. Of those that a mesh axis runs over, the one named last changes fastest.
Arguments:
- queries: bfloat16 [8192, 512], P('ctx', 'head'), may hold values from -6 to 6
- keys: bfloat16 [8192, 512], P('ctx', 'head'), may hold values from -6 to 6
- values: bfloat16 [8192, 512], P('ctx', 'head'), may hold values from -6 to 6
- write_rates: float32 [4, 8192], P('head', 'ctx'), may hold values from 0 to 2, as said below
- norm_gain: float32 [128], replicated, may hold values from 0.1 to 1.9
- w_out: bfloat16 [512, 2048], P(None, 'head'), may hold values from -0.25 to 0.25
Outputs:
- mixed: bfloat16 [8192, 2048], P('ctx', 'head')
Inputs may be any that keep to these rules, and one draw needn't show every extreme that they name: `write_rates`: every rate lies strictly between 0 and 2.
All inputs are finite; a program needn't handle non-finite values.
Results may differ from a plain program's by a relative error of at most 0.0049.
Values may be sent and summed in bfloat16 or wider, within the bound.
A program may use at most 64 MiB of HBM per device.

v0:
```python
import jax
import jax.numpy as jnp
from jax import lax
from jax.sharding import PartitionSpec as P

HEAD_DIM = 128
GROUP = 128


def passed_along(value, axis, steps):
    count = lax.axis_size(axis)
    leading, last = (max(0, -steps), min(count, count - steps))
    return lax.ppermute(value, axis, [(source, source + steps) for source in range(leading, last)])


def matmul(left, right):
    return jnp.dot(left, right, precision=lax.Precision.HIGHEST, preferred_element_type=jnp.float32)


def unit_rows(matrix):
    wide = matrix.astype(jnp.float32)
    return wide / jnp.sqrt(jnp.sum(wide * wide, axis=-1, keepdims=True) + 1e-06)


def block_parts(query_block, key_block, value_block, rate_block):
    width = key_block.shape[1]
    gram = matmul(key_block, key_block.T)
    lower = jnp.tril(rate_block[:, None] * gram, -1) + jnp.eye(
        key_block.shape[0], dtype=jnp.float32
    )
    stacked = jnp.concatenate(
        [rate_block[:, None] * key_block, rate_block[:, None] * value_block], axis=1
    )
    solved = jax.scipy.linalg.solve_triangular(lower, stacked, lower=True, unit_diagonal=True)
    wy_keys = solved[:, :width]
    wy_values = solved[:, width:]
    transition = jnp.eye(width, dtype=jnp.float32) - matmul(wy_keys.T, key_block)
    offset = matmul(wy_values.T, key_block)
    scores = jnp.tril(matmul(query_block, key_block.T))
    return (wy_keys, wy_values, transition, offset, scores)


def block_output(state, query_block, wy_keys, wy_values, transition, offset, scores):
    result = matmul(query_block, state.T) + matmul(scores, wy_values - matmul(wy_keys, state.T))
    return (result, matmul(state, transition) + offset)


def shards(queries, keys, values, write_rates, norm_gain, w_out):
    length = queries.shape[0]
    blocks = length // GROUP
    query_rows = unit_rows(queries).reshape(blocks, GROUP, HEAD_DIM)
    key_rows = unit_rows(keys).reshape(blocks, GROUP, HEAD_DIM)
    value_rows = values.astype(jnp.float32).reshape(blocks, GROUP, HEAD_DIM)
    rate_rows = write_rates[0].reshape(blocks, GROUP)
    wy_keys, wy_values, transition, offset, scores = jax.vmap(block_parts)(
        query_rows, key_rows, value_rows, rate_rows
    )
    identity_hd = jnp.eye(HEAD_DIM, dtype=jnp.float32)
    zero_state = jnp.zeros((HEAD_DIM, HEAD_DIM), jnp.float32)

    def compose(carry, step):
        return ((matmul(carry[0], step[0]), matmul(carry[1], step[0]) + step[1]), None)

    (device_map, device_offset), unused = lax.scan(
        compose, (identity_hd, zero_state), (transition, offset)
    )

    def relay(step, state):
        return passed_along(matmul(state, device_map) + device_offset, "ctx", 1)

    start_state = lax.fori_loop(0, lax.axis_size("ctx") - 1, relay, zero_state)

    def advance(state, block):
        result, state = block_output(state, *block)
        return (state, result)

    final, outputs = lax.scan(
        advance, start_state, (query_rows, wy_keys, wy_values, transition, offset, scores)
    )
    outputs = outputs.reshape(length, HEAD_DIM)
    normed = (
        outputs * lax.rsqrt(jnp.mean(outputs * outputs, axis=-1, keepdims=True) + 1e-06) * norm_gain
    ).astype(jnp.bfloat16)
    token_rows = lax.all_to_all(normed, "head", split_axis=0, concat_axis=1, tiled=True)
    full_rows = jnp.dot(
        token_rows,
        lax.all_gather(w_out, "head", axis=1, tiled=True),
        preferred_element_type=jnp.float32,
    ).astype(jnp.bfloat16)
    return lax.all_to_all(full_rows, "head", split_axis=1, concat_axis=0, tiled=True)


def solution(mesh):
    return jax.shard_map(
        shards,
        mesh=mesh,
        in_specs=(
            P("ctx", "head"),
            P("ctx", "head"),
            P("ctx", "head"),
            P("head", "ctx"),
            P(),
            P(None, "head"),
        ),
        out_specs=P("ctx", "head"),
        check_vma=False,
    )
```

profile of v0, /device:TPU:25, one launch (start us, length us, event | category | flops | bytes accessed | tf_op | source)
XLA Modules:
  0.0 203.9 jit_solution(2503386418949848491)
XLA Ops:
  7.3 1.2 fusion.36
  8.5 1.2 convert_divide_fusion.1
  9.8 1.9 fusion.31
  11.8 78.6 %custom-call.4 = f32[8,1,128,128]{2,3,1,0:T(8,128)S(1)} custom-call(f32[8,1,128,128]{3,2,1,0:T(8,128)S(1)} %fusion.31), custom_call_target="InvertDiagBlocksLowerTriangular" | custom-call | tf_op jit(solution)/shard_map/vmap(jit(_solve_triangular))/triangular_solve | solution.py:34
  94.8 5.2 %while.40 = (s32[]{:T(128)}, f32[128,128]{0,1:T(8,128)S(1)}, f32[128,128]{0,1:T(8,128)S(1)}, f32[8,128,128]{2,1,0:T(8,128)S(1)}, f32[8,128,128]{1,2,0:T(8,128)S(1)}) while((s32[]{:T(128)}, f32[128,128]{0,1:T(8,128)S(1)}, f32[128,128]{0,1:T(8,128)S(1)}, f32[8,128,128]{2,1,0:T(8,128)S(1)}, ...), condition=%wide.region_2.3_spmd.clone.clone, body=%wide.region_1.0_spmd.clone.sunk.clone | while | flops 50364416 | bytes 721995 | solution.py:64
  100.2 43.2 %while.38 = (s32[]{:T(128)}, f32[128,128]{1,0:T(8,128)S(1)}, f32[128,128]{1,0:T(8,128)S(1)}, f32[128,128]{1,0:T(8,128)S(1)}) while((s32[]{:T(128)}, f32[128,128]{1,0:T(8,128)S(1)}, f32[128,128]{1,0:T(8,128)S(1)}, f32[128,128]{1,0:T(8,128)S(1)}) %tuple.75), condition=%wide.region_4.5_spmd.clone, body=%wide.region_3.4_spmd.sunk.clone | while | flops 25182208 | bytes 524381 | solution.py:71
  100.4 3.1 %collective-permute-start = (f32[128,128]{1,0:T(8,128)S(1)}, f32[128,128]{1,0:T(8,128)S(1)}, u32[]{:S(2)}, u32[]{:S(2)}) collective-permute-start(f32[128,128]{1,0:T(8,128)S(1)} %convolution_add_fusion.4), channel_id=1, source_target_pairs={{0,4},{4,8},{8,12},{12,16},{16,20},{20,24},{24,28},{1,5},{5,9},{9,... | collective-permute-start | bytes 196616 | tf_op jit(solution)/shard_map/while/body/eval_jaxpr/ppermute | solution.py:13
  103.6 2.8 %collective-permute-done = f32[128,128]{1,0:T(8,128)S(1)} collective-permute-done((f32[128,128]{1,0:T(8,128)S(1)}, f32[128,128]{1,0:T(8,128)S(1)}, u32[]{:S(2)}, u32[]{:S(2)}) %collective-permute-start) | collective-permute-done | bytes 65568 | tf_op jit(solution)/shard_map/while/body/eval_jaxpr/ppermute | solution.py:13
  106.5 2.2 %collective-permute-start = (f32[128,128]{1,0:T(8,128)S(1)}, f32[128,128]{1,0:T(8,128)S(1)}, u32[]{:S(2)}, u32[]{:S(2)}) collective-permute-start(f32[128,128]{1,0:T(8,128)S(1)} %convolution_add_fusion.4), channel_id=1, source_target_pairs={{0,4},{4,8},{8,12},{12,16},{16,20},{20,24},{24,28},{1,5},{5,9},{9,... | collective-permute-start | bytes 196616 | tf_op jit(solution)/shard_map/while/body/eval_jaxpr/ppermute | solution.py:13
  108.8 3.7 %collective-permute-done = f32[128,128]{1,0:T(8,128)S(1)} collective-permute-done((f32[128,128]{1,0:T(8,128)S(1)}, f32[128,128]{1,0:T(8,128)S(1)}, u32[]{:S(2)}, u32[]{:S(2)}) %collective-permute-start) | collective-permute-done | bytes 65568 | tf_op jit(solution)/shard_map/while/body/eval_jaxpr/ppermute | solution.py:13
  112.7 1.9 collective-permute-start
  114.6 4.0 %collective-permute-done = f32[128,128]{1,0:T(8,128)S(1)} collective-permute-done((f32[128,128]{1,0:T(8,128)S(1)}, f32[128,128]{1,0:T(8,128)S(1)}, u32[]{:S(2)}, u32[]{:S(2)}) %collective-permute-start) | collective-permute-done | bytes 65568 | tf_op jit(solution)/shard_map/while/body/eval_jaxpr/ppermute | solution.py:13
  118.8 1.9 collective-permute-start
  120.7 4.0 %collective-permute-done = f32[128,128]{1,0:T(8,128)S(1)} collective-permute-done((f32[128,128]{1,0:T(8,128)S(1)}, f32[128,128]{1,0:T(8,128)S(1)}, u32[]{:S(2)}, u32[]{:S(2)}) %collective-permute-start) | collective-permute-done | bytes 65568 | tf_op jit(solution)/shard_map/while/body/eval_jaxpr/ppermute | solution.py:13
  124.9 1.9 collective-permute-start
  126.8 4.0 %collective-permute-done = f32[128,128]{1,0:T(8,128)S(1)} collective-permute-done((f32[128,128]{1,0:T(8,128)S(1)}, f32[128,128]{1,0:T(8,128)S(1)}, u32[]{:S(2)}, u32[]{:S(2)}) %collective-permute-start) | collective-permute-done | bytes 65568 | tf_op jit(solution)/shard_map/while/body/eval_jaxpr/ppermute | solution.py:13
  131.0 1.9 collective-permute-start
  133.0 4.3 %collective-permute-done = f32[128,128]{1,0:T(8,128)S(1)} collective-permute-done((f32[128,128]{1,0:T(8,128)S(1)}, f32[128,128]{1,0:T(8,128)S(1)}, u32[]{:S(2)}, u32[]{:S(2)}) %collective-permute-start) | collective-permute-done | bytes 65568 | tf_op jit(solution)/shard_map/while/body/eval_jaxpr/ppermute | solution.py:13
  137.5 1.9 collective-permute-start
  139.4 4.0 %collective-permute-done = f32[128,128]{1,0:T(8,128)S(1)} collective-permute-done((f32[128,128]{1,0:T(8,128)S(1)}, f32[128,128]{1,0:T(8,128)S(1)}, u32[]{:S(2)}, u32[]{:S(2)}) %collective-permute-start) | collective-permute-done | bytes 65568 | tf_op jit(solution)/shard_map/while/body/eval_jaxpr/ppermute | solution.py:13
  143.9 1.2 convolution_select_fusion
  145.1 14.8 %while.39 = (s32[]{:T(128)}, f32[128,128]{0,1:T(8,128)S(1)}, f32[8,128,128]{2,1,0:T(8,128)S(1)}, f32[8,128,128]{2,1,0:T(8,128)S(1)}, f32[8,128,128]{1,2,0:T(8,12...) while((s32[]{:T(128)}, f32[128,128]{0,1:T(8,128)S(1)}, ...), condition=%wide.region_7.8_spmd.clone, body=%wide.region_6.7_spmd.sunk.clone | while | flops 100712448 | bytes 1117281 | solution.py:77
  145.2 1.1 convolution_subtract_fusion.4
  147.0 1.1 convolution_subtract_fusion.4
  148.9 1.1 convolution_subtract_fusion.4
  152.5 1.1 convolution_subtract_fusion.4
  154.4 1.1 convolution_subtract_fusion.4
  156.2 1.1 convolution_subtract_fusion.4
  158.1 1.1 convolution_subtract_fusion.4
  160.4 16.3 %all_to_all.35 = bf16[4,256,128]{2,1,0:T(8,128)(2,1)S(1)} all-to-all(bf16[4,256,128]{2,1,0:T(8,128)(2,1)S(1)} %fusion.39), channel_id=1, replica_groups=mesh['ctx'=8,'head'=4] {'head'}, dimensions={0} | all-to-all | bytes 524288 | tf_op jit(solution)/shard_map/all_to_all | solution.py:84
  176.9 2.3 %convolution_convert_fusion = bf16[256,2048]{1,0:T(8,128)(2,1)S(1)} fusion(bf16[256,512]{0,1:T(8,128)(2,1)S(1)} %bitcast.150, bf16[512,2048]{1,0:T(8,128)(2,1)} %all-gather.2.cloned.1.call-done), kind=kOutput, calls=%fused_computation.33 | convolution fusion | flops 537395200 | bytes 3407872 | tf_op jit(solution)/shard_map/dot_general | solution.py:85
  179.3 16.9 %all_to_all.36 = bf16[256,4,512]{2,0,1:T(8,128)(2,1)S(1)} all-to-all(bf16[256,4,512]{2,0,1:T(8,128)(2,1)S(1)} %bitcast.144), channel_id=1, replica_groups=mesh['ctx'=8,'head'=4] {'head'}, dimensions={1} | all-to-all | bytes 2097152 | tf_op jit(solution)/shard_map/all_to_all | solution.py:90
  (110 shorter events, 20.6 us)
Async XLA Ops:
  6.5 83.8 %copy-start.2 = (f32[1,1024]{1,0:T(1,128)S(1)}, f32[1,1024]{1,0:T(1,128)}, u32[]{:S(2)}) copy-start(f32[1,1024]{1,0:T(1,128)} %param.15) | copy-start | bytes 12292
  6.5 83.8 %copy-start.1 = (bf16[1024,128]{1,0:T(8,128)(2,1)S(1)}, bf16[1024,128]{1,0:T(8,128)(2,1)}, u32[]{:S(2)}) copy-start(bf16[1024,128]{1,0:T(8,128)(2,1)} %param.14) | copy-start | bytes 786436
  6.5 170.3 %all-gather.2.cloned.1.call-start = ((), (), s32[]{:S(2)}) async-start(), calls=%async_computation.2 | async-start | bytes 2621440 | tf_op jit(solution)/shard_map/all_gather | solution.py:87
  94.8 48.7 %copy-start = (bf16[1024,128]{1,0:T(8,128)(2,1)S(1)}, bf16[1024,128]{1,0:T(8,128)(2,1)}, u32[]{:S(2)}) copy-start(bf16[1024,128]{1,0:T(8,128)(2,1)} %param.12) | copy-start | bytes 786436
  100.4 5.9 %collective-permute-start = (f32[128,128]{1,0:T(8,128)S(1)}, f32[128,128]{1,0:T(8,128)S(1)}, u32[]{:S(2)}, u32[]{:S(2)}) collective-permute-start(f32[128,128]{1,0:T(8,128)S(1)} %convolution_add_fusion.4), channel_id=1, source_target_pairs={{0,4},{4,8},{8,12},{12,16},{16,20},{20,24},{24,28},{1,5},{5,9},{9,... | collective-permute-start | bytes 196616 | tf_op jit(solution)/shard_map/while/body/eval_jaxpr/ppermute | solution.py:13
  106.5 5.9 %collective-permute-start = (f32[128,128]{1,0:T(8,128)S(1)}, f32[128,128]{1,0:T(8,128)S(1)}, u32[]{:S(2)}, u32[]{:S(2)}) collective-permute-start(f32[128,128]{1,0:T(8,128)S(1)} %convolution_add_fusion.4), channel_id=1, source_target_pairs={{0,4},{4,8},{8,12},{12,16},{16,20},{20,24},{24,28},{1,5},{5,9},{9,... | collective-permute-start | bytes 196616 | tf_op jit(solution)/shard_map/while/body/eval_jaxpr/ppermute | solution.py:13
  112.7 5.9 %collective-permute-start = (f32[128,128]{1,0:T(8,128)S(1)}, f32[128,128]{1,0:T(8,128)S(1)}, u32[]{:S(2)}, u32[]{:S(2)}) collective-permute-start(f32[128,128]{1,0:T(8,128)S(1)} %convolution_add_fusion.4), channel_id=1, source_target_pairs={{0,4},{4,8},{8,12},{12,16},{16,20},{20,24},{24,28},{1,5},{5,9},{9,... | collective-permute-start | bytes 196616 | tf_op jit(solution)/shard_map/while/body/eval_jaxpr/ppermute | solution.py:13
  118.8 5.9 %collective-permute-start = (f32[128,128]{1,0:T(8,128)S(1)}, f32[128,128]{1,0:T(8,128)S(1)}, u32[]{:S(2)}, u32[]{:S(2)}) collective-permute-start(f32[128,128]{1,0:T(8,128)S(1)} %convolution_add_fusion.4), channel_id=1, source_target_pairs={{0,4},{4,8},{8,12},{12,16},{16,20},{20,24},{24,28},{1,5},{5,9},{9,... | collective-permute-start | bytes 196616 | tf_op jit(solution)/shard_map/while/body/eval_jaxpr/ppermute | solution.py:13
  124.9 5.9 %collective-permute-start = (f32[128,128]{1,0:T(8,128)S(1)}, f32[128,128]{1,0:T(8,128)S(1)}, u32[]{:S(2)}, u32[]{:S(2)}) collective-permute-start(f32[128,128]{1,0:T(8,128)S(1)} %convolution_add_fusion.4), channel_id=1, source_target_pairs={{0,4},{4,8},{8,12},{12,16},{16,20},{20,24},{24,28},{1,5},{5,9},{9,... | collective-permute-start | bytes 196616 | tf_op jit(solution)/shard_map/while/body/eval_jaxpr/ppermute | solution.py:13
  131.0 6.2 %collective-permute-start = (f32[128,128]{1,0:T(8,128)S(1)}, f32[128,128]{1,0:T(8,128)S(1)}, u32[]{:S(2)}, u32[]{:S(2)}) collective-permute-start(f32[128,128]{1,0:T(8,128)S(1)} %convolution_add_fusion.4), channel_id=1, source_target_pairs={{0,4},{4,8},{8,12},{12,16},{16,20},{20,24},{24,28},{1,5},{5,9},{9,... | collective-permute-start | bytes 196616 | tf_op jit(solution)/shard_map/while/body/eval_jaxpr/ppermute | solution.py:13
  137.5 5.9 %collective-permute-start = (f32[128,128]{1,0:T(8,128)S(1)}, f32[128,128]{1,0:T(8,128)S(1)}, u32[]{:S(2)}, u32[]{:S(2)}) collective-permute-start(f32[128,128]{1,0:T(8,128)S(1)} %convolution_add_fusion.4), channel_id=1, source_target_pairs={{0,4},{4,8},{8,12},{12,16},{16,20},{20,24},{24,28},{1,5},{5,9},{9,... | collective-permute-start | bytes 196616 | tf_op jit(solution)/shard_map/while/body/eval_jaxpr/ppermute | solution.py:13
  145.1 15.0 %copy-start.3 = (f32[128]{0:T(128)S(1)}, f32[128]{0:T(128)}, u32[]{:S(2)}) copy-start(f32[128]{0:T(128)} %param.16) | copy-start | bytes 1540
Sparse Core Ops, SparseCore 0:
  8.9 24.0 all-gather.1
where the time goes:
time: 205 us; the launch traced here: 204 us
  other arithmetic  82.1 us (40%)
  blocking collectives  33.1 us (16%)
  matrix products  28.9 us (14%)
  waiting for transfers between devices  27.4 us (13%)
  starting transfers between devices  15 us (7%)
  between operations  13.7 us (7%)
  local copies, waits for them, and re-layouts  2.82 us (1%)
    another operation x3, other arithmetic, block_parts(): jax.scipy.linalg.solve_triangular(lower, stacked, lower=True, unit_diagon...  78.7 us
    ppermute x7, waiting for transfers between devices, passed_along(): lax.ppermute(value, axis, [(source, source + steps) for source in range(l...  26.6 us
    dot_general x59, matrix products, matmul(): jnp.dot(left, right, precision=lax.Precision.HIGHEST, preferred_element_t...  25.6 us
    all_to_all x1, blocking collectives, shards(): lax.all_to_all(full_rows, 'head', split_axis=1, concat_axis=0, tiled=True)  16.9 us
    all_to_all x1, blocking collectives, shards(): lax.all_to_all(normed, 'head', split_axis=0, concat_axis=1, tiled=True)  16.3 us
    ppermute x7, starting transfers between devices, passed_along(): lax.ppermute(value, axis, [(source, source + steps) for source in range(l...  15 us
  transfers between devices with their start and end apart: 8, of which 7 were waited for; matrix products, arithmetic and copies ran while one was open for 54% of the time, Pallas kernels for 0%

commit v1 on v0

v1 whole, which is shorter than its diff:
```python
import functools

import jax
import jax.numpy as jnp
from jax import lax
from jax.experimental import pallas as pl
from jax.experimental.pallas import tpu as pltpu
from jax.sharding import PartitionSpec as P

F32 = jnp.float32
BF16 = jnp.bfloat16
MESH = pl.DeviceIdType.MESH
GROUP = 128
CHUNKS = 4


def halves(wide):
    high = wide.astype(BF16)
    return high, (wide - high.astype(F32)).astype(BF16)


def dot(left, right):
    return jnp.dot(left, right, preferred_element_type=F32)


def dot_rows(left, right):
    return lax.dot_general(left, right, (((1,), (1,)), ((), ())), preferred_element_type=F32)


def beside(*parts):
    return jnp.concatenate(parts, axis=1)


def above(*parts):
    return jnp.concatenate(parts, axis=0)


def dot_wide(left, right):
    left_high, left_low = halves(left)
    right_high, right_low = halves(right)
    return dot(beside(left_high, left_low, left_high), above(right_high, right_high, right_low))


def kernel(
    count,
    heads,
    q_ref,
    k_ref,
    v_ref,
    rate_ref,
    gain_ref,
    w_ref,
    out_ref,
    inverse,
    lower,
    writes,
    moves,
    prefix,
    eff_high,
    eff_low,
    local,
    pair,
    state_in,
    state_out,
    gathered,
    pair_send,
    pair_recv,
    state_send,
    state_recv,
    out_send,
    forward_send,
    out_recv,
):
    ctx = lax.axis_index("ctx")
    head = lax.axis_index("head")
    side = lax.rem(ctx, 2)
    place = ctx // 2
    places = count // 2
    mate = ctx + 1 - 2 * side
    core = lax.rem(head, 2)
    chip = head // 2
    chips = heads // 2
    twin = head + 1 - 2 * core
    length, width = q_ref.shape
    blocks = length // GROUP

    barrier = pltpu.get_barrier_semaphore()

    def greet(to_ctx, to_head):
        pl.semaphore_signal(barrier, inc=1, device_id=(to_ctx, to_head), device_id_type=MESH)

    def chip_at(step):
        return lax.rem(chip + step, chips)

    greet(mate, head)
    greet(ctx, twin)
    for step in range(1, chips):
        greet(ctx, chip_at(step) * 2 + core)

    @pl.when(place > 0)
    def _():
        greet(ctx - 2, head)

    @pl.when(place < places - 1)
    def _():
        greet(ctx + 2, head)

    row = lax.broadcasted_iota(jnp.int32, (GROUP, GROUP), 0)
    col = lax.broadcasted_iota(jnp.int32, (GROUP, GROUP), 1)
    eye = (row == col).astype(F32)

    rates = above(*[rate_ref[0:1, b * GROUP : (b + 1) * GROUP] for b in range(blocks)])
    rate_cols = rates.T
    key_rows = []

    def part(ref, b):
        return ref[b * GROUP : (b + 1) * GROUP, :]

    for b in range(blocks):
        key = part(k_ref, b)
        wide = key.astype(F32)
        gram = dot_rows(key, key)
        scale_col = lax.rsqrt(jnp.sum(wide * wide, axis=1, keepdims=True) + 1e-06)
        scale_row = lax.rsqrt(jnp.sum(gram * eye, axis=0, keepdims=True) + 1e-06)
        key_rows.append(scale_row)
        strict = jnp.where(
            row > col, gram * (rate_cols[:, b : b + 1] * scale_col) * scale_row, 0.0
        )
        lower[b] = strict
        near = (row // 2 == col // 2) & (row != col)
        inverse[b] = eye - jnp.where(near, strict, 0.0)

    span = 2
    while span < GROUP:
        corner = (row // (2 * span) == col // (2 * span)) & (row // span != col // span)
        for b in range(blocks):
            held = inverse[b]
            inverse[b] = held - dot_wide(
                held, dot_wide(jnp.where(corner, lower[b], 0.0), held)
            )
        span *= 2

    for b in range(blocks):
        key = part(k_ref, b)
        value = part(v_ref, b)
        wide = key.astype(F32)
        scale_col = lax.rsqrt(jnp.sum(wide * wide, axis=1, keepdims=True) + 1e-06)
        spread = inverse[b] * rates[b : b + 1, :]
        key_high, key_low = halves(spread * key_rows[b])
        value_high, value_low = halves(spread)
        written = beside(
            dot(beside(key_high, key_low), above(key, key)),
            dot(beside(value_high, value_low), above(value, value)),
        )
        writes[b] = written
        high, low = halves(written * scale_col)
        turned = key.T
        moved = dot(beside(turned, turned), above(high, low))
        moves[b] = beside(eye - moved[:, :width], moved[:, width:])

    nothing = jnp.zeros((GROUP, width), F32)
    run = beside(eye, nothing)
    for b in range(blocks):
        prefix[b] = run
        step = moves[b]
        if b == 0:
            run = step
        else:
            run = dot_wide(step[:, :width], run) + beside(nothing, step[:, width:])
    pair[side] = run

    pl.semaphore_wait(
        barrier,
        2
        + (chips - 1)
        + (place > 0).astype(jnp.int32)
        + (place < places - 1).astype(jnp.int32),
    )
    swap = pltpu.make_async_remote_copy(
        src_ref=pair.at[side],
        dst_ref=pair.at[side],
        send_sem=pair_send,
        recv_sem=pair_recv,
        device_id=(mate, head),
        device_id_type=MESH,
    )
    swap.start()

    for b in range(blocks):
        query = part(q_ref, b)
        wide = query.astype(F32)
        scale_col = lax.rsqrt(jnp.sum(wide * wide, axis=1, keepdims=True) + 1e-06)
        scores = dot_rows(query, part(k_ref, b))
        scores = jnp.where(row >= col, scores * scale_col * key_rows[b], 0.0)
        seen = dot_wide(scores, writes[b])
        asked = wide * scale_col - seen[:, :width]
        both = dot_wide(asked, prefix[b])
        high, low = halves(both[:, :width])
        rows = slice(b * GROUP, (b + 1) * GROUP)
        eff_high[rows, :] = high
        eff_low[rows, :] = low
        local[rows, :] = both[:, width:] + seen[:, width:]

    swap.wait_recv()
    first = pair[0]
    second = pair[1]
    joined = dot_wide(second[:, :width], first) + beside(nothing, second[:, width:])

    relay = pltpu.make_async_remote_copy(
        src_ref=state_out,
        dst_ref=state_in,
        send_sem=state_send,
        recv_sem=state_recv,
        device_id=(lax.rem(ctx + 2, count), head),
        device_id_type=MESH,
    )

    @pl.when(place == 0)
    def _():
        state_in[...] = nothing
        state_out[...] = joined[:, width:]

    @pl.when(place > 0)
    def _():
        relay.wait_recv()
        state_out[...] = dot_wide(joined[:, :width], state_in[...]) + joined[:, width:]

    @pl.when(place < places - 1)
    def _():
        relay.start()

    start = state_in[...]
    start = jnp.where(
        side == 0, start, dot_wide(first[:, :width], start) + first[:, width:]
    )
    start_high, start_low = halves(start)
    start_all = above(start_high, start_high, start_low)

    size = length // CHUNKS
    gain = gain_ref[...]

    def out_copy(slot, chunk, send_sem, to_head):
        view = gathered.at[slot, pl.ds(chunk * size, size), :]
        return pltpu.make_async_remote_copy(
            src_ref=view,
            dst_ref=view,
            send_sem=send_sem,
            recv_sem=out_recv.at[chunk, slot],
            device_id=(ctx, to_head),
            device_id_type=MESH,
        )

    sent = []
    for chunk in range(CHUNKS):
        rows = slice(chunk * size, (chunk + 1) * size)
        high = eff_high[rows, :]
        result = dot(beside(high, eff_low[rows, :], high), start_all) + local[rows, :]
        power = jnp.mean(result * result, axis=1, keepdims=True)
        gathered[head, rows, :] = (result * lax.rsqrt(power + 1e-06) * gain).astype(BF16)
        for step in range(1, chips):
            copy = out_copy(head, chunk, out_send.at[chunk, step], chip_at(step) * 2 + core)
            copy.start()
            sent.append(copy)
        copy = out_copy(head, chunk, out_send.at[chunk, 0], twin)
        copy.start()
        sent.append(copy)

    def finish(chunk):
        rows = slice(chunk * size, (chunk + 1) * size)
        out_copy(twin, chunk, out_send.at[chunk, 0], twin).wait_recv()
        for step in range(1, chips):
            slot = chip_at(step) * 2 + 1 - core
            out_copy(slot, chunk, forward_send.at[chunk, step], twin).wait_recv()
        joined_rows = beside(*[gathered[slot, rows, :] for slot in range(heads)])
        out_ref[rows, :] = dot(joined_rows, w_ref[...]).astype(BF16)

    for chunk in range(CHUNKS):
        for step in range(1, chips):
            slot = chip_at(step) * 2 + core
            copy = out_copy(slot, chunk, forward_send.at[chunk, step], twin)
            copy.wait_recv()
            copy.start()
            sent.append(copy)
        if chunk > 0:
            finish(chunk - 1)
    finish(CHUNKS - 1)

    for copy in sent:
        copy.wait_send()
    swap.wait_send()

    @pl.when(place < places - 1)
    def _():
        relay.wait_send()


def solution(mesh):
    count, heads = mesh.shape["ctx"], mesh.shape["head"]

    def shards(queries, keys, values, write_rates, norm_gain, w_out):
        length, width = queries.shape
        blocks = length // GROUP
        vmem = pl.BlockSpec(memory_space=pltpu.VMEM)
        wide = (blocks, GROUP, 2 * width)
        return pl.pallas_call(
            functools.partial(kernel, count, heads),
            out_shape=jax.ShapeDtypeStruct((length, w_out.shape[1]), BF16),
            in_specs=[vmem] * 6,
            out_specs=vmem,
            scratch_shapes=[
                pltpu.VMEM((blocks, GROUP, GROUP), F32),
                pltpu.VMEM((blocks, GROUP, GROUP), F32),
                pltpu.VMEM(wide, F32),
                pltpu.VMEM(wide, F32),
                pltpu.VMEM(wide, F32),
                pltpu.VMEM((length, width), BF16),
                pltpu.VMEM((length, width), BF16),
                pltpu.VMEM((length, width), F32),
                pltpu.VMEM((2, GROUP, 2 * width), F32),
                pltpu.VMEM((width, width), F32),
                pltpu.VMEM((width, width), F32),
                pltpu.VMEM((heads, length, width), BF16),
                pltpu.SemaphoreType.DMA,
                pltpu.SemaphoreType.DMA,
                pltpu.SemaphoreType.DMA,
                pltpu.SemaphoreType.DMA,
                pltpu.SemaphoreType.DMA((CHUNKS, heads // 2)),
                pltpu.SemaphoreType.DMA((CHUNKS, heads // 2)),
                pltpu.SemaphoreType.DMA((CHUNKS, heads)),
            ],
            compiler_params=pltpu.CompilerParams(collective_id=0, has_side_effects=True),
        )(queries, keys, values, write_rates, norm_gain.reshape(1, width), w_out)

    return jax.shard_map(
        shards,
        mesh=mesh,
        in_specs=(
            P("ctx", "head"),
            P("ctx", "head"),
            P("ctx", "head"),
            P("head", "ctx"),
            P(),
            P(None, "head"),
        ),
        out_specs=P("ctx", "head"),
        check_vma=False,
    )
```

time: 205 us -> 39.4 us (0.19)
  other arithmetic: 82.1 us -> 0 us
  Pallas kernels: 0 us -> 36.9 us
  blocking collectives: 33.1 us -> 0 us
  matrix products: 28.9 us -> 0 us
  waiting for transfers between devices: 27.4 us -> 0 us
  starting transfers between devices: 15 us -> 0 us
  between operations: 13.7 us -> 0.01 us
    another operation x3 -> x0, other arithmetic: 78.7 us -> none  [block_parts(): jax.scipy.linalg.solve_triangular(lower, stacked, lower=True, unit_diagon...]
    pallas_call x0 -> x1, Pallas kernels: none -> 36.9 us  [shards(): pl.pallas_call(functools.partial(kernel, count, heads), out_shape=jax.Sha...]
    all_to_all x2 -> x0, blocking collectives: 33.1 us -> none  [the longest x1 16.9 us: shards(): lax.all_to_all(full_rows, 'head', split_axis=1, concat_axis=0, tiled=True)]
    dot_general x60 -> x0, matrix products: 27.9 us -> none  [the longest x59 25.6 us: matmul(): jnp.dot(left, right, precision=lax.Precision.HIGHEST, preferred_element_t...]
    ppermute x7 -> x0, waiting for transfers between devices: 26.6 us -> none  [passed_along(): lax.ppermute(value, axis, [(source, source + steps) for source in range(l...]
    ppermute x7 -> x0, starting transfers between devices: 15 us -> none  [passed_along(): lax.ppermute(value, axis, [(source, source + steps) for source in range(l...]
  transfers between devices with their start and end apart: 8 -> 0, of which waited for: 7 -> 0; matrix products, arithmetic and copies ran while one was open for 54% -> 0% of each run, Pallas kernels for 0% -> 0%
where the time goes in v1:
time: 39.4 us; the launch traced here: 39.2 us
  Pallas kernels  36.9 us (94%)
  local copies, waits for them, and re-layouts  2.26 us (6%)
    pallas_call x1, Pallas kernels, shards(): pl.pallas_call(functools.partial(kernel, count, heads), out_shape=jax.Sha...  36.9 us
    unnamed x1, local copies, waits for them, and re-layouts  2.26 us

profile of v1, /device:TPU:25, one launch (start us, length us, event | category | flops | bytes accessed | tf_op | source)
XLA Modules:
  0.0 39.2 jit_solution(15836895140120212404)
XLA Ops:
  0.0 36.9 %shard_map.64 = bf16[1024,512]{1,0:T(8,128)(2,1)} custom-call(bf16[1024,128]{1,0:T(8,128)(2,1)} %q_ref.1, bf16[1024,128]{1,0:T(8,128)(2,1)} %k_ref.1, bf16[1024,128]{1,0:T(8,128)(2,1)} %v_ref.1, f32[1,1024]{1,0:T(1,128)} %rate_ref.1, f32[1,128]{1,0:T(1,128)} %bitcast.1, bf16[512,512]{1,0:T(8,128)(2,1)} %w_ref.1), custom_call_target="tpu_custom_call" | custom-call | tf_op jit(solution)/shard_map/pallas_call | solution.py:305
  36.9 2.3 %copy.8 = bf16[1024,512]{1,0:T(8,128)(2,1)} copy(bf16[1024,512]{1,0:T(8,128)(2,1)} %shard_map.64) | data formatting | bytes 2097152

commit v2 on v1

v2 whole, which is shorter than its diff:
```python
import functools

import jax
import jax.numpy as jnp
from jax import lax
from jax.experimental import pallas as pl
from jax.experimental.pallas import tpu as pltpu
from jax.sharding import PartitionSpec as P

F32 = jnp.float32
BF16 = jnp.bfloat16
MESH = pl.DeviceIdType.MESH
GROUP = 128
CHUNKS = 4
ROUNDS = 2


def halves(wide):
    high = wide.astype(BF16)
    return high, (wide - high.astype(F32)).astype(BF16)


def dot(left, right):
    return jnp.dot(left, right, preferred_element_type=F32)


def dot_rows(left, right):
    return lax.dot_general(left, right, (((1,), (1,)), ((), ())), preferred_element_type=F32)


def beside(*parts):
    return jnp.concatenate(parts, axis=1)


def above(*parts):
    return jnp.concatenate(parts, axis=0)


def dot_wide(left, right):
    left_high, left_low = halves(left)
    right_high, right_low = halves(right)
    return dot(beside(left_high, left_low, left_high), above(right_high, right_high, right_low))


def dot_rows_wide(left, right):
    left_high, left_low = halves(left)
    right_high, right_low = halves(right)
    return dot_rows(beside(left_high, left_low, left_high), beside(right_high, right_high, right_low))


def kernel(
    count,
    heads,
    q_ref,
    k_ref,
    v_ref,
    rate_ref,
    parts,
    states,
    inverse,
    lower,
    writes,
    pair,
    state_in,
    state_out,
    pair_send,
    pair_recv,
    relay_send,
    relay_recv,
    part_send,
    part_pass,
    part_recv,
    state_send,
    state_pass,
    state_recv,
):
    ctx = lax.axis_index("ctx")
    head = lax.axis_index("head")
    side = lax.rem(ctx, 2)
    place = ctx // 2
    places = count // 2
    mate = ctx + 1 - 2 * side
    core = lax.rem(head, 2)
    chip = head // 2
    chips = heads // 2
    twin = head + 1 - 2 * core
    length, width = q_ref.shape
    blocks = length // GROUP
    chunks = parts.shape[1]
    size = length // chunks

    barrier = pltpu.get_barrier_semaphore()

    def greet(to_ctx, to_head):
        pl.semaphore_signal(barrier, inc=1, device_id=(to_ctx, to_head), device_id_type=MESH)

    def chip_at(step):
        return lax.rem(chip + step, chips)

    greet(mate, head)
    greet(ctx, twin)
    for step in range(1, chips):
        greet(ctx, chip_at(step) * 2 + core)

    @pl.when(place > 0)
    def _():
        greet(ctx - 2, head)

    @pl.when(place < places - 1)
    def _():
        greet(ctx + 2, head)

    row = lax.broadcasted_iota(jnp.int32, (GROUP, GROUP), 0)
    col = lax.broadcasted_iota(jnp.int32, (GROUP, GROUP), 1)
    eye = (row == col).astype(F32)

    rates = above(*[rate_ref[0:1, b * GROUP : (b + 1) * GROUP] for b in range(blocks)])
    rate_cols = rates.T
    key_rows = []
    moves = []

    def part(ref, b):
        return ref[b * GROUP : (b + 1) * GROUP, :]

    for b in range(blocks):
        key = part(k_ref, b)
        wide = key.astype(F32)
        gram = dot_rows(key, key)
        scale_col = lax.rsqrt(jnp.sum(wide * wide, axis=1, keepdims=True) + 1e-06)
        scale_row = lax.rsqrt(jnp.sum(gram * eye, axis=0, keepdims=True) + 1e-06)
        key_rows.append(scale_row)
        strict = jnp.where(
            row > col, gram * (rate_cols[:, b : b + 1] * scale_col) * scale_row, 0.0
        )
        lower[b] = strict
        near = (row // 2 == col // 2) & (row != col)
        inverse[b] = eye - jnp.where(near, strict, 0.0)

    span = 2
    while span < GROUP:
        corner = (row // (2 * span) == col // (2 * span)) & (row // span != col // span)
        for b in range(blocks):
            held = inverse[b]
            inverse[b] = held - dot_wide(
                held, dot_wide(jnp.where(corner, lower[b], 0.0), held)
            )
        span *= 2

    for b in range(blocks):
        key = part(k_ref, b)
        value = part(v_ref, b)
        wide = key.astype(F32)
        scale_col = lax.rsqrt(jnp.sum(wide * wide, axis=1, keepdims=True) + 1e-06)
        spread = inverse[b] * rates[b : b + 1, :]
        key_high, key_low = halves(spread * key_rows[b])
        value_high, value_low = halves(spread)
        written = beside(
            dot(beside(key_high, key_low), above(key, key)),
            dot(beside(value_high, value_low), above(value, value)),
        )
        writes[b] = written
        high, low = halves(written * scale_col)
        turned = key.T
        moved = dot(beside(turned, turned), above(high, low))
        moves.append(beside(eye - moved[:, :width], moved[:, width:]))

    nothing = jnp.zeros((GROUP, width), F32)

    def after(later, earlier):
        return dot_wide(later[:, :width], earlier) + beside(nothing, later[:, width:])

    ranges = {(b, b + 1): moves[b] for b in range(blocks)}
    reach = 1
    while reach < blocks:
        for b in range(0, blocks, 2 * reach):
            middle, end = min(b + reach, blocks), min(b + 2 * reach, blocks)
            if middle < end:
                ranges[b, end] = after(ranges[middle, end], ranges[b, middle])
        reach *= 2
    pair[side] = ranges[0, blocks]

    pl.semaphore_wait(
        barrier,
        2
        + (chips - 1)
        + (place > 0).astype(jnp.int32)
        + (place < places - 1).astype(jnp.int32),
    )
    swap = pltpu.make_async_remote_copy(
        src_ref=pair.at[side],
        dst_ref=pair.at[side],
        send_sem=pair_send,
        recv_sem=pair_recv,
        device_id=(mate, head),
        device_id_type=MESH,
    )
    swap.start()

    for b in range(1, blocks):
        if (0, b) not in ranges:
            low = b & -b
            ranges[0, b] = after(ranges[b - low, b], ranges[0, b - low])

    def part_copy(slot, chunk, send_sem, to_head):
        return pltpu.make_async_remote_copy(
            src_ref=parts.at[slot, chunk],
            dst_ref=parts.at[slot, chunk],
            send_sem=send_sem,
            recv_sem=part_recv.at[chunk, slot],
            device_id=(ctx, to_head),
            device_id_type=MESH,
        )

    def state_copy(slot, send_sem, to_head):
        return pltpu.make_async_remote_copy(
            src_ref=states.at[slot],
            dst_ref=states.at[slot],
            send_sem=send_sem,
            recv_sem=state_recv.at[slot],
            device_id=(ctx, to_head),
            device_id_type=MESH,
        )

    sent = []
    for b in range(blocks):
        query = part(q_ref, b)
        wide = query.astype(F32)
        scale_col = lax.rsqrt(jnp.sum(wide * wide, axis=1, keepdims=True) + 1e-06)
        scores = dot_rows(query, part(k_ref, b))
        scores = jnp.where(row >= col, scores * scale_col * key_rows[b], 0.0)
        seen = dot_wide(scores, writes[b])
        asked = wide * scale_col - seen[:, :width]
        if b == 0:
            both = beside(asked, nothing)
        else:
            both = dot_wide(asked, ranges[0, b])
        chunk, at = divmod(b * GROUP, size)
        parts[head, chunk, 0, at : at + GROUP, :] = both[:, :width].astype(BF16)
        parts[head, chunk, 1, at : at + GROUP, :] = (both[:, width:] + seen[:, width:]).astype(BF16)
        if at + GROUP == size:
            for step in range(1, chips):
                copy = part_copy(head, chunk, part_send.at[chunk, step], chip_at(step) * 2 + core)
                copy.start()
                sent.append(copy)
            copy = part_copy(head, chunk, part_send.at[chunk, 0], twin)
            copy.start()
            sent.append(copy)

    swap.wait_recv()
    first = pair[0]
    second = pair[1]
    joined = after(second, first)
    joined_map = joined[:, :width]
    joined_add = joined[:, width:].T

    rounds = state_in.shape[0]
    tall = width // rounds

    def relay(turn):
        return pltpu.make_async_remote_copy(
            src_ref=state_out.at[turn],
            dst_ref=state_in.at[turn],
            send_sem=relay_send.at[turn],
            recv_sem=relay_recv.at[turn],
            device_id=(lax.rem(ctx + 2, count), head),
            device_id_type=MESH,
        )

    for turn in range(rounds):
        rows = slice(turn * tall, (turn + 1) * tall)

        @pl.when(place == 0)
        def _():
            state_in[turn] = jnp.zeros((tall, width), F32)
            state_out[turn] = joined_add[rows, :]

        @pl.when(place > 0)
        def _():
            relay(turn).wait_recv()

            @pl.when(place < places - 1)
            def _():
                state_out[turn] = dot_rows_wide(state_in[turn], joined_map) + joined_add[rows, :]

        @pl.when(place < places - 1)
        def _():
            relay(turn).start()

    start = state_in[...].reshape(width, width)
    states[head] = jnp.where(
        side == 0, start, dot_rows_wide(start, first[:, :width]) + first[:, width:].T
    )
    for step in range(1, chips):
        copy = state_copy(head, state_send.at[step], chip_at(step) * 2 + core)
        copy.start()
        sent.append(copy)
    copy = state_copy(head, state_send.at[0], twin)
    copy.start()
    sent.append(copy)

    for chunk in range(chunks):
        for step in range(1, chips):
            slot = chip_at(step) * 2 + core
            copy = part_copy(slot, chunk, part_pass.at[chunk, step], twin)
            copy.wait_recv()
            copy.start()
            sent.append(copy)
    for step in range(1, chips):
        slot = chip_at(step) * 2 + core
        copy = state_copy(slot, state_pass.at[step], twin)
        copy.wait_recv()
        copy.start()
        sent.append(copy)

    for chunk in range(chunks):
        part_copy(twin, chunk, part_send.at[chunk, 0], twin).wait_recv()
        for step in range(1, chips):
            slot = chip_at(step) * 2 + 1 - core
            part_copy(slot, chunk, part_pass.at[chunk, step], twin).wait_recv()
    state_copy(twin, state_send.at[0], twin).wait_recv()
    for step in range(1, chips):
        slot = chip_at(step) * 2 + 1 - core
        state_copy(slot, state_pass.at[step], twin).wait_recv()

    for copy in sent:
        copy.wait_send()
    swap.wait_send()

    @pl.when(place < places - 1)
    def _():
        for turn in range(rounds):
            relay(turn).wait_send()


def finish(parts, states, gain_ref, w_ref, out_ref):
    heads = parts.shape[0]
    gain = gain_ref[...]
    rows = []
    for slot in range(heads):
        high, low = halves(states[slot])
        asked = parts[slot, 0, 0]
        result = dot_rows(beside(asked, asked), beside(high, low)) + parts[slot, 0, 1].astype(F32)
        power = jnp.mean(result * result, axis=1, keepdims=True)
        rows.append((result * lax.rsqrt(power + 1e-06) * gain).astype(BF16))
    out_ref[...] = dot(beside(*rows), w_ref[...]).astype(BF16)


def solution(mesh):
    count, heads = mesh.shape["ctx"], mesh.shape["head"]

    def shards(queries, keys, values, write_rates, norm_gain, w_out):
        length, width = queries.shape
        blocks = length // GROUP
        size = length // CHUNKS
        columns = w_out.shape[1]
        vmem = pl.BlockSpec(memory_space=pltpu.VMEM)
        parts, states = pl.pallas_call(
            functools.partial(kernel, count, heads),
            out_shape=(
                jax.ShapeDtypeStruct((heads, CHUNKS, 2, size, width), BF16),
                jax.ShapeDtypeStruct((heads, width, width), F32),
            ),
            in_specs=[vmem] * 4,
            out_specs=(vmem, vmem),
            scratch_shapes=[
                pltpu.VMEM((blocks, GROUP, GROUP), F32),
                pltpu.VMEM((blocks, GROUP, GROUP), F32),
                pltpu.VMEM((blocks, GROUP, 2 * width), F32),
                pltpu.VMEM((2, GROUP, 2 * width), F32),
                pltpu.VMEM((ROUNDS, width // ROUNDS, width), F32),
                pltpu.VMEM((ROUNDS, width // ROUNDS, width), F32),
                pltpu.SemaphoreType.DMA,
                pltpu.SemaphoreType.DMA,
                pltpu.SemaphoreType.DMA((ROUNDS,)),
                pltpu.SemaphoreType.DMA((ROUNDS,)),
                pltpu.SemaphoreType.DMA((CHUNKS, heads // 2)),
                pltpu.SemaphoreType.DMA((CHUNKS, heads // 2)),
                pltpu.SemaphoreType.DMA((CHUNKS, heads)),
                pltpu.SemaphoreType.DMA((heads // 2,)),
                pltpu.SemaphoreType.DMA((heads // 2,)),
                pltpu.SemaphoreType.DMA((heads,)),
            ],
            compiler_params=pltpu.CompilerParams(
                collective_id=0, has_side_effects=True, vmem_limit_bytes=24 << 20
            ),
        )(queries, keys, values, write_rates)
        return pl.pallas_call(
            finish,
            out_shape=jax.ShapeDtypeStruct((length, columns), BF16),
            grid=(CHUNKS,),
            in_specs=[
                pl.BlockSpec((heads, 1, 2, size, width), lambda i: (0, i, 0, 0, 0)),
                pl.BlockSpec((heads, width, width), lambda i: (0, 0, 0)),
                pl.BlockSpec((1, width), lambda i: (0, 0)),
                pl.BlockSpec(w_out.shape, lambda i: (0, 0)),
            ],
            out_specs=pl.BlockSpec((size, columns), lambda i: (i, 0)),
            compiler_params=pltpu.CompilerParams(vmem_limit_bytes=24 << 20),
        )(parts, states, norm_gain.reshape(1, width), w_out)

    return jax.shard_map(
        shards,
        mesh=mesh,
        in_specs=(
            P("ctx", "head"),
            P("ctx", "head"),
            P("ctx", "head"),
            P("head", "ctx"),
            P(),
            P(None, "head"),
        ),
        out_specs=P("ctx", "head"),
        check_vma=False,
    )
```

time: 39.4 us -> 39.4 us (level)
  Pallas kernels: 36.9 us -> 33.9 us
  local copies, waits for them, and re-layouts: 2.26 us -> 5.23 us
    pallas_call x1 -> x2, Pallas kernels: 36.9 us -> 33.9 us  [the longest x1 30.7 us: shards(): pl.pallas_call(functools.partial(kernel, count, heads), out_shape=(jax.Sh...]
    unnamed x1 -> x12, local copies, waits for them, and re-layouts: 2.26 us -> 5.23 us
where the time goes in v2:
time: 39.4 us; the launch traced here: 39.1 us
  Pallas kernels  33.9 us (86%)
  local copies, waits for them, and re-layouts  5.23 us (13%)
    pallas_call x1, Pallas kernels, shards(): pl.pallas_call(functools.partial(kernel, count, heads), out_shape=(jax.Sh...  30.7 us
    unnamed x12, local copies, waits for them, and re-layouts  5.23 us
    pallas_call x1, Pallas kernels, shards(): pl.pallas_call(finish, out_shape=jax.ShapeDtypeStruct((length, columns),...  3.19 us

profile of v2, /device:TPU:25, one launch (start us, length us, event | category | flops | bytes accessed | tf_op | source)
XLA Modules:
  0.0 39.1 jit_solution(5923594389277316676)
XLA Ops:
  0.0 0.0 copy-start.1
  0.0 0.9 %copy-done.1 = bf16[1024,128]{1,0:T(8,128)(2,1)S(1)} copy-done((bf16[1024,128]{1,0:T(8,128)(2,1)S(1)}, bf16[1024,128]{1,0:T(8,128)(2,1)}, u32[]{:S(2)}) %copy-start.1) | copy-done | bytes 262168
  1.0 0.0 copy-start.2
  1.0 0.9 %copy-done.2 = bf16[1024,128]{1,0:T(8,128)(2,1)S(1)} copy-done((bf16[1024,128]{1,0:T(8,128)(2,1)S(1)}, bf16[1024,128]{1,0:T(8,128)(2,1)}, u32[]{:S(2)}) %copy-start.2) | copy-done | bytes 262168
  1.9 0.0 copy-start.3
  1.9 0.9 %copy-done.3 = bf16[1024,128]{1,0:T(8,128)(2,1)S(1)} copy-done((bf16[1024,128]{1,0:T(8,128)(2,1)S(1)}, bf16[1024,128]{1,0:T(8,128)(2,1)}, u32[]{:S(2)}) %copy-start.3) | copy-done | bytes 262168
  2.9 0.0 copy-start.4
  2.9 0.7 %copy-done.4 = f32[1,1024]{1,0:T(1,128)S(1)} copy-done((f32[1,1024]{1,0:T(1,128)S(1)}, f32[1,1024]{1,0:T(1,128)}, u32[]{:S(2)}) %copy-start.4) | copy-done | bytes 4120
  3.5 30.7 %shard_map.64 = (bf16[4,4,2,256,128]{4,3,2,1,0:T(8,128)(2,1)S(1)}, f32[4,128,128]{2,1,0:T(8,128)S(1)}) custom-call(bf16[1024,128]{1,0:T(8,128)(2,1)S(1)} %copy-done.1, bf16[1024,128]{1,0:T(8,128)(2,1)S(1)} %copy-done.2, bf16[1024,128]{1,0:T(8,128)(2,1)S(1)} %copy-done.3, f32[1,1024]{1,0:T(1,128)S(1)} %copy-done.4), custom_call_target="tpu_custom_call" | custom-call | tf_op jit(solution)/shard_map/pallas_call | solution.py:357
  34.2 0.0 copy-start
  34.2 1.0 %copy-done = bf16[512,512]{1,0:T(8,128)(2,1)S(1)} copy-done((bf16[512,512]{1,0:T(8,128)(2,1)S(1)}, bf16[512,512]{1,0:T(8,128)(2,1)}, u32[]{:S(2)}) %copy-start) | copy-done | bytes 524312
  35.3 0.0 copy-start.5
  35.3 0.7 %copy-done.5 = f32[128]{0:T(128)S(1)} copy-done((f32[128]{0:T(128)S(1)}, f32[128]{0:T(128)}, u32[]{:S(2)}) %copy-start.5) | copy-done | bytes 536
  35.9 3.2 %shard_map.65 = bf16[1024,512]{1,0:T(8,128)(2,1)} custom-call(bf16[4,4,2,256,128]{4,3,2,1,0:T(8,128)(2,1)S(1)} %get-tuple-element.7.parts, f32[4,128,128]{2,1,0:T(8,128)S(1)} %get-tuple-element.8.states, f32[1,128]{1,0:T(1,128)S(1)} %bitcast.1, bf16[512,512]{1,0:T(8,128)(2,1)S(1)} %copy-done), custom_call_target="tpu_custom_call" | custom-call | tf_op jit(solution)/shard_map/pallas_call | solution.py:387
Async XLA Ops:
  0.0 0.9 %copy-start.1 = (bf16[1024,128]{1,0:T(8,128)(2,1)S(1)}, bf16[1024,128]{1,0:T(8,128)(2,1)}, u32[]{:S(2)}) copy-start(bf16[1024,128]{1,0:T(8,128)(2,1)} %q_ref.1) | copy-start | bytes 786436
  1.0 0.9 %copy-start.2 = (bf16[1024,128]{1,0:T(8,128)(2,1)S(1)}, bf16[1024,128]{1,0:T(8,128)(2,1)}, u32[]{:S(2)}) copy-start(bf16[1024,128]{1,0:T(8,128)(2,1)} %k_ref.1) | copy-start | bytes 786436
  1.9 0.9 %copy-start.3 = (bf16[1024,128]{1,0:T(8,128)(2,1)S(1)}, bf16[1024,128]{1,0:T(8,128)(2,1)}, u32[]{:S(2)}) copy-start(bf16[1024,128]{1,0:T(8,128)(2,1)} %v_ref.1) | copy-start | bytes 786436
  2.9 0.7 %copy-start.4 = (f32[1,1024]{1,0:T(1,128)S(1)}, f32[1,1024]{1,0:T(1,128)}, u32[]{:S(2)}) copy-start(f32[1,1024]{1,0:T(1,128)} %rate_ref.1) | copy-start | bytes 12292
  34.2 1.0 %copy-start = (bf16[512,512]{1,0:T(8,128)(2,1)S(1)}, bf16[512,512]{1,0:T(8,128)(2,1)}, u32[]{:S(2)}) copy-start(bf16[512,512]{1,0:T(8,128)(2,1)} %w_ref.1) | copy-start | bytes 1572868
  35.3 0.7 %copy-start.5 = (f32[128]{0:T(128)S(1)}, f32[128]{0:T(128)}, u32[]{:S(2)}) copy-start(f32[128]{0:T(128)} %param.10) | copy-start | bytes 1540

commit v3 on v2

--- a/solution.py
+++ b/solution.py
@@ -51,18 +51,28 @@
 def kernel(
     count,
     heads,
+    q_hbm,
+    k_hbm,
+    v_hbm,
+    rate_hbm,
+    gain_hbm,
+    w_hbm,
+    parts,
+    states,
+    gain_out,
+    w_out,
     q_ref,
     k_ref,
     v_ref,
     rate_ref,
-    parts,
-    states,
     inverse,
+    coarse,
     lower,
     writes,
     pair,
     state_in,
     state_out,
+    load_sem,
     pair_send,
     pair_recv,
     relay_send,
@@ -89,6 +99,21 @@
     chunks = parts.shape[1]
     size = length // chunks
 
+    loads = [
+        pltpu.make_async_copy(source, target, load_sem.at[at])
+        for at, (source, target) in enumerate(
+            (
+                (k_hbm, k_ref),
+                (rate_hbm, rate_ref),
+                (v_hbm, v_ref),
+                (q_hbm, q_ref),
+                (w_hbm, w_out),
+                (gain_hbm, gain_out),
+            )
+        )
+    ]
+    for load in loads:
+        load.start()
     barrier = pltpu.get_barrier_semaphore()
 
     def greet(to_ctx, to_head):
@@ -114,6 +139,8 @@
     col = lax.broadcasted_iota(jnp.int32, (GROUP, GROUP), 1)
     eye = (row == col).astype(F32)
 
+    loads[0].wait()
+    loads[1].wait()
     rates = above(*[rate_ref[0:1, b * GROUP : (b + 1) * GROUP] for b in range(blocks)])
     rate_cols = rates.T
     key_rows = []
@@ -133,25 +160,45 @@
             row > col, gram * (rate_cols[:, b : b + 1] * scale_col) * scale_row, 0.0
         )
         lower[b] = strict
+        coarse[b] = strict.astype(BF16)
         near = (row // 2 == col // 2) & (row != col)
-        inverse[b] = eye - jnp.where(near, strict, 0.0)
+        inverse[b] = (eye - jnp.where(near, strict, 0.0)).astype(BF16)
 
     span = 2
     while span < GROUP:
-        corner = (row // (2 * span) == col // (2 * span)) & (row // span != col // span)
+        corner = (
+            ((row // (2 * span) == col // (2 * span)) & (row // span != col // span))
+            .astype(F32)
+            .astype(BF16)
+        )
+        spots = [slice(at, at + span) for at in range(span, GROUP, 2 * span)]
+        if span < 16:
+            spots = [slice(0, GROUP)]
         for b in range(blocks):
             held = inverse[b]
-            inverse[b] = held - dot_wide(
-                held, dot_wide(jnp.where(corner, lower[b], 0.0), held)
-            )
+            rows = above(*[held[spot, :] for spot in spots])
+            change = dot(dot(rows, coarse[b] * corner).astype(BF16), held).astype(BF16)
+            rows = rows - change
+            at = 0
+            for spot in spots:
+                tall = spot.stop - spot.start
+                inverse[b, spot, :] = rows[at : at + tall, :]
+                at += tall
         span *= 2
 
+    loads[2].wait()
     for b in range(blocks):
         key = part(k_ref, b)
         value = part(v_ref, b)
         wide = key.astype(F32)
         scale_col = lax.rsqrt(jnp.sum(wide * wide, axis=1, keepdims=True) + 1e-06)
-        spread = inverse[b] * rates[b : b + 1, :]
+        held = inverse[b]
+        high, low = halves(lower[b])
+        miss = eye - held.astype(F32) - dot(beside(high, low), above(held, held))
+        rough = miss.astype(BF16)
+        miss = miss + dot(rough, rough)
+        exact = held.astype(F32) + dot(held, miss.astype(BF16))
+        spread = exact * rates[b : b + 1, :]
         key_high, key_low = halves(spread * key_rows[b])
         value_high, value_low = halves(spread)
         written = beside(
@@ -196,6 +243,7 @@
     )
     swap.start()
 
+    loads[3].wait()
     for b in range(1, blocks):
         if (0, b) not in ranges:
             low = b & -b
@@ -325,6 +373,8 @@
     for copy in sent:
         copy.wait_send()
     swap.wait_send()
+    loads[4].wait()
+    loads[5].wait()
 
     @pl.when(place < places - 1)
     def _():
@@ -332,17 +382,29 @@
             relay(turn).wait_send()
 
 
-def finish(parts, states, gain_ref, w_ref, out_ref):
-    heads = parts.shape[0]
+def finish(parts, states, gain_ref, w_ref, out_ref, staged, sems):
+    heads, chunks = parts.shape[:2]
+    size, width = parts.shape[3:]
     gain = gain_ref[...]
-    rows = []
-    for slot in range(heads):
-        high, low = halves(states[slot])
-        asked = parts[slot, 0, 0]
-        result = dot_rows(beside(asked, asked), beside(high, low)) + parts[slot, 0, 1].astype(F32)
-        power = jnp.mean(result * result, axis=1, keepdims=True)
-        rows.append((result * lax.rsqrt(power + 1e-06) * gain).astype(BF16))
-    out_ref[...] = dot(beside(*rows), w_ref[...]).astype(BF16)
+    share = jnp.full((2 * width, width), 1.0 / width, BF16)
+    starts = [beside(*halves(states[slot])) for slot in range(heads)]
+    copies = []
+    for chunk in range(chunks):
+        rows = []
+        for slot in range(heads):
+            asked = parts[slot, chunk, 0]
+            result = dot_rows(beside(asked, asked), starts[slot])
+            result = result + parts[slot, chunk, 1].astype(F32)
+            power = dot(beside(*halves(result * result)), share)
+            rows.append((result * lax.rsqrt(power + 1e-06) * gain).astype(BF16))
+        staged[chunk] = dot(beside(*rows), w_ref[...]).astype(BF16)
+        copy = pltpu.make_async_copy(
+            staged.at[chunk], out_ref.at[pl.ds(chunk * size, size), :], sems.at[chunk]
+        )
+        copy.start()
+        copies.append(copy)
+    for copy in copies:
+        copy.wait()
 
 
 def solution(mesh):
@@ -354,21 +416,30 @@
         size = length // CHUNKS
         columns = w_out.shape[1]
         vmem = pl.BlockSpec(memory_space=pltpu.VMEM)
-        parts, states = pl.pallas_call(
+        hbm = pl.BlockSpec(memory_space=pltpu.MemorySpace.HBM)
+        parts, states, gain, weights = pl.pallas_call(
             functools.partial(kernel, count, heads),
             out_shape=(
                 jax.ShapeDtypeStruct((heads, CHUNKS, 2, size, width), BF16),
                 jax.ShapeDtypeStruct((heads, width, width), F32),
+                jax.ShapeDtypeStruct((1, width), F32),
+                jax.ShapeDtypeStruct(w_out.shape, BF16),
             ),
-            in_specs=[vmem] * 4,
-            out_specs=(vmem, vmem),
+            in_specs=[hbm] * 6,
+            out_specs=(vmem,) * 4,
             scratch_shapes=[
-                pltpu.VMEM((blocks, GROUP, GROUP), F32),
+                pltpu.VMEM((length, width), BF16),
+                pltpu.VMEM((length, width), BF16),
+                pltpu.VMEM((length, width), BF16),
+                pltpu.VMEM((1, length), F32),
+                pltpu.VMEM((blocks, GROUP, GROUP), BF16),
+                pltpu.VMEM((blocks, GROUP, GROUP), BF16),
                 pltpu.VMEM((blocks, GROUP, GROUP), F32),
                 pltpu.VMEM((blocks, GROUP, 2 * width), F32),
                 pltpu.VMEM((2, GROUP, 2 * width), F32),
                 pltpu.VMEM((ROUNDS, width // ROUNDS, width), F32),
                 pltpu.VMEM((ROUNDS, width // ROUNDS, width), F32),
+                pltpu.SemaphoreType.DMA((6,)),
                 pltpu.SemaphoreType.DMA,
                 pltpu.SemaphoreType.DMA,
                 pltpu.SemaphoreType.DMA((ROUNDS,)),
@@ -383,20 +454,21 @@
             compiler_params=pltpu.CompilerParams(
                 collective_id=0, has_side_effects=True, vmem_limit_bytes=24 << 20
             ),
-        )(queries, keys, values, write_rates)
+        )(*[
+            pltpu.with_memory_space_constraint(given, pltpu.MemorySpace.HBM)
+            for given in (queries, keys, values, write_rates, norm_gain.reshape(1, width), w_out)
+        ])
         return pl.pallas_call(
             finish,
             out_shape=jax.ShapeDtypeStruct((length, columns), BF16),
-            grid=(CHUNKS,),
-            in_specs=[
-                pl.BlockSpec((heads, 1, 2, size, width), lambda i: (0, i, 0, 0, 0)),
-                pl.BlockSpec((heads, width, width), lambda i: (0, 0, 0)),
-                pl.BlockSpec((1, width), lambda i: (0, 0)),
-                pl.BlockSpec(w_out.shape, lambda i: (0, 0)),
+            in_specs=[vmem] * 4,
+            out_specs=pl.BlockSpec(memory_space=pltpu.MemorySpace.HBM),
+            scratch_shapes=[
+                pltpu.VMEM((CHUNKS, size, columns), BF16),
+                pltpu.SemaphoreType.DMA((CHUNKS,)),
             ],
-            out_specs=pl.BlockSpec((size, columns), lambda i: (i, 0)),
             compiler_params=pltpu.CompilerParams(vmem_limit_bytes=24 << 20),
-        )(parts, states, norm_gain.reshape(1, width), w_out)
+        )(parts, states, gain, weights)
 
     return jax.shard_map(
         shards,

time: 39.4 us -> 29.9 us (0.76)
  local copies, waits for them, and re-layouts: 5.23 us -> 0 us
  Pallas kernels: 33.9 us -> 29.8 us
    unnamed x12 -> x0, local copies, waits for them, and re-layouts: 5.23 us -> none
    pallas_call x1, Pallas kernels: 30.7 us -> 26.6 us  [shards(): pl.pallas_call(functools.partial(kernel, count, heads), out_shape=(jax.Sh...]
where the time goes in v3:
time: 29.9 us; the launch traced here: 29.8 us
  Pallas kernels  29.8 us (100%)
    pallas_call x1, Pallas kernels, shards(): pl.pallas_call(functools.partial(kernel, count, heads), out_shape=(jax.Sh...  26.6 us
    pallas_call x1, Pallas kernels, shards(): pl.pallas_call(finish, out_shape=jax.ShapeDtypeStruct((length, columns),...  3.16 us

profile of v3, /device:TPU:25, one launch (start us, length us, event | category | flops | bytes accessed | tf_op | source)
XLA Modules:
  0.0 29.8 jit_solution(17602336719329113786)
XLA Ops:
  0.0 26.6 %shard_map.64 = (bf16[4,4,2,256,128]{4,3,2,1,0:T(8,128)(2,1)S(1)}, f32[4,128,128]{2,1,0:T(8,128)S(1)}, f32[1,128]{1,0:T(1,128)S(1)}, bf16[512,512]{1,0:T(8,128)(2,1)S(1)}) custom-call(bf16[1024,128]{1,0:T(8,128)(2,1)} %q_hbm.1, bf16[1024,128]{1,0:T(8,128)(2,1)} %k_hbm.1, bf16[1024,128]{1,0:T(8,128)(2,1)} %v_hbm.1, f32[1,1024]{1,0:T(1,128)} %rate_hbm.1, ...), custom_call_target="tpu_custom_call" | custom-call | tf_op jit(solution)/shard_map/pallas_call | solution.py:420
  26.6 3.2 %shard_map.65 = bf16[1024,512]{1,0:T(8,128)(2,1)} custom-call(bf16[4,4,2,256,128]{4,3,2,1,0:T(8,128)(2,1)S(1)} %get-tuple-element.9.parts, f32[4,128,128]{2,1,0:T(8,128)S(1)} %get-tuple-element.10.states, f32[1,128]{1,0:T(1,128)S(1)} %get-tuple-element.11.gain_ref, bf16[512,512]{1,0:T(8,128)(2,1)S(1)} %get-tuple-element.12.w_ref), custom_call_target="tpu_custom_call" | custom-call | tf_op jit(solution)/shard_map/pallas_call | solution.py:461

commit v4 on v3

--- a/solution.py
+++ b/solution.py
@@ -46,6 +46,13 @@
     left_high, left_low = halves(left)
     right_high, right_low = halves(right)
     return dot_rows(beside(left_high, left_low, left_high), beside(right_high, right_high, right_low))
+
+
+def settled(parts, slot, chunk, start, gain, share):
+    asked = parts[slot, chunk, 0]
+    result = dot_rows(beside(asked, asked), start) + parts[slot, chunk, 1].astype(F32)
+    power = dot(beside(*halves(result * result)), share)
+    return (result * lax.rsqrt(power + 1e-06) * gain).astype(BF16)
 
 
 def kernel(
@@ -61,6 +68,7 @@
     states,
     gain_out,
     w_out,
+    done,
     q_ref,
     k_ref,
     v_ref,
@@ -69,6 +77,7 @@
     coarse,
     lower,
     writes,
+    mine,
     pair,
     state_in,
     state_out,
@@ -346,13 +355,34 @@
     copy.start()
     sent.append(copy)
 
-    for chunk in range(chunks):
+    def pass_on(chunk):
         for step in range(1, chips):
             slot = chip_at(step) * 2 + core
             copy = part_copy(slot, chunk, part_pass.at[chunk, step], twin)
             copy.wait_recv()
             copy.start()
             sent.append(copy)
+
+    for chunk in range(chunks - 1):
+        pass_on(chunk)
+
+    loads[4].wait()
+    loads[5].wait()
+    gain = gain_out[...]
+    share = jnp.full((2 * width, width), 1.0 / width, BF16)
+    own_start = beside(*halves(states[head]))
+    for chunk in range(chunks):
+        mine[core, chunk] = settled(parts, head, chunk, own_start, gain, share)
+    state_copy(twin, state_send.at[0], twin).wait_recv()
+    twin_start = beside(*halves(states[twin]))
+    for chunk in range(chunks):
+        part_copy(twin, chunk, part_send.at[chunk, 0], twin).wait_recv()
+        mine[1 - core, chunk] = settled(parts, twin, chunk, twin_start, gain, share)
+    pass_on(chunks - 1)
+    own_weights = w_out[pl.ds(pl.multiple_of(chip * 2 * width, 2 * width), 2 * width), :]
+    for chunk in range(chunks):
+        done[chunk] = dot(beside(mine[0, chunk], mine[1, chunk]), own_weights)
+
     for step in range(1, chips):
         slot = chip_at(step) * 2 + core
         copy = state_copy(slot, state_pass.at[step], twin)
@@ -361,11 +391,9 @@
         sent.append(copy)
 
     for chunk in range(chunks):
-        part_copy(twin, chunk, part_send.at[chunk, 0], twin).wait_recv()
         for step in range(1, chips):
             slot = chip_at(step) * 2 + 1 - core
             part_copy(slot, chunk, part_pass.at[chunk, step], twin).wait_recv()
-    state_copy(twin, state_send.at[0], twin).wait_recv()
     for step in range(1, chips):
         slot = chip_at(step) * 2 + 1 - core
         state_copy(slot, state_pass.at[step], twin).wait_recv()
@@ -373,8 +401,6 @@
     for copy in sent:
         copy.wait_send()
     swap.wait_send()
-    loads[4].wait()
-    loads[5].wait()
 
     @pl.when(place < places - 1)
     def _():
@@ -382,22 +408,21 @@
             relay(turn).wait_send()
 
 
-def finish(parts, states, gain_ref, w_ref, out_ref, staged, sems):
+def finish(parts, states, gain_ref, w_ref, done, out_ref, staged, sems):
     heads, chunks = parts.shape[:2]
     size, width = parts.shape[3:]
+    chip, chips = lax.axis_index("head") // 2, heads // 2
     gain = gain_ref[...]
     share = jnp.full((2 * width, width), 1.0 / width, BF16)
-    starts = [beside(*halves(states[slot])) for slot in range(heads)]
+    slots = [lax.rem(chip + step, chips) * 2 + side for step in range(1, chips) for side in range(2)]
+    starts = [beside(*halves(states[slot])) for slot in slots]
+    weights = above(*[w_ref[pl.ds(pl.multiple_of(slot * width, width), width), :] for slot in slots])
     copies = []
     for chunk in range(chunks):
-        rows = []
-        for slot in range(heads):
-            asked = parts[slot, chunk, 0]
-            result = dot_rows(beside(asked, asked), starts[slot])
-            result = result + parts[slot, chunk, 1].astype(F32)
-            power = dot(beside(*halves(result * result)), share)
-            rows.append((result * lax.rsqrt(power + 1e-06) * gain).astype(BF16))
-        staged[chunk] = dot(beside(*rows), w_ref[...]).astype(BF16)
+        rows = [
+            settled(parts, slot, chunk, start, gain, share) for slot, start in zip(slots, starts)
+        ]
+        staged[chunk] = (done[chunk] + dot(beside(*rows), weights)).astype(BF16)
         copy = pltpu.make_async_copy(
             staged.at[chunk], out_ref.at[pl.ds(chunk * size, size), :], sems.at[chunk]
         )
@@ -417,16 +442,17 @@
         columns = w_out.shape[1]
         vmem = pl.BlockSpec(memory_space=pltpu.VMEM)
         hbm = pl.BlockSpec(memory_space=pltpu.MemorySpace.HBM)
-        parts, states, gain, weights = pl.pallas_call(
+        parts, states, gain, weights, done = pl.pallas_call(
             functools.partial(kernel, count, heads),
             out_shape=(
                 jax.ShapeDtypeStruct((heads, CHUNKS, 2, size, width), BF16),
                 jax.ShapeDtypeStruct((heads, width, width), F32),
                 jax.ShapeDtypeStruct((1, width), F32),
                 jax.ShapeDtypeStruct(w_out.shape, BF16),
+                jax.ShapeDtypeStruct((CHUNKS, size, columns), F32),
             ),
             in_specs=[hbm] * 6,
-            out_specs=(vmem,) * 4,
+            out_specs=(vmem,) * 5,
             scratch_shapes=[
                 pltpu.VMEM((length, width), BF16),
                 pltpu.VMEM((length, width), BF16),
@@ -436,6 +462,7 @@
                 pltpu.VMEM((blocks, GROUP, GROUP), BF16),
                 pltpu.VMEM((blocks, GROUP, GROUP), F32),
                 pltpu.VMEM((blocks, GROUP, 2 * width), F32),
+                pltpu.VMEM((2, CHUNKS, size, width), BF16),
                 pltpu.VMEM((2, GROUP, 2 * width), F32),
                 pltpu.VMEM((ROUNDS, width // ROUNDS, width), F32),
                 pltpu.VMEM((ROUNDS, width // ROUNDS, width), F32),
@@ -461,14 +488,14 @@
         return pl.pallas_call(
             finish,
             out_shape=jax.ShapeDtypeStruct((length, columns), BF16),
-            in_specs=[vmem] * 4,
+            in_specs=[vmem] * 5,
             out_specs=pl.BlockSpec(memory_space=pltpu.MemorySpace.HBM),
             scratch_shapes=[
                 pltpu.VMEM((CHUNKS, size, columns), BF16),
                 pltpu.SemaphoreType.DMA((CHUNKS,)),
             ],
             compiler_params=pltpu.CompilerParams(vmem_limit_bytes=24 << 20),
-        )(parts, states, gain, weights)
+        )(parts, states, gain, weights, done)
 
     return jax.shard_map(
         shards,

time: 29.9 us -> 29.4 us (0.983)
  Pallas kernels: 29.8 us -> 29.3 us
    pallas_call x1, Pallas kernels: 3.16 us -> 2.69 us  [shards(): pl.pallas_call(finish, out_shape=jax.ShapeDtypeStruct((length, columns),...]
where the time goes in v4:
time: 29.4 us; the launch traced here: 29.3 us
  Pallas kernels  29.3 us (100%)
    pallas_call x1, Pallas kernels, shards(): pl.pallas_call(functools.partial(kernel, count, heads), out_shape=(jax.Sh...  26.6 us
    pallas_call x1, Pallas kernels, shards(): pl.pallas_call(finish, out_shape=jax.ShapeDtypeStruct((length, columns),...  2.69 us

profile of v4, /device:TPU:25, one launch (start us, length us, event | category | flops | bytes accessed | tf_op | source)
XLA Modules:
  0.0 29.3 jit_solution(2579234429187571863)
XLA Ops:
  0.0 26.6 %shard_map.64 = (bf16[4,4,2,256,128]{4,3,2,1,0:T(8,128)(2,1)S(1)}, f32[4,128,128]{2,1,0:T(8,128)S(1)}, f32[1,128]{1,0:T(1,128)S(1)}, bf16[512,512]{1,0:T(8,128)(2,1)S(1)}, f32[4,256,512]{2,1,0:T(8,128)S(1)}) custom-call(bf16[1024,128]{1,0:T(8,128)(2,1)} %q_hbm.1, bf16[1024,128]{1,0:T(8,128)(2,1)} %k_hbm.1, bf16[1024,128]{1,0:T(8,128)(2,1)} %v_hbm.1, ...), custom_call_target="tpu_custom_call" | custom-call | tf_op jit(solution)/shard_map/pallas_call | solution.py:445
  26.6 2.7 %shard_map.65 = bf16[1024,512]{1,0:T(8,128)(2,1)} custom-call(bf16[4,4,2,256,128]{4,3,2,1,0:T(8,128)(2,1)S(1)} %get-tuple-element.10.parts, f32[4,128,128]{2,1,0:T(8,128)S(1)} %get-tuple-element.11.states, f32[1,128]{1,0:T(1,128)S(1)} %get-tuple-element.12.gain_ref, bf16[512,512]{1,0:T(8,128)(2,1)S(1)} %get-tuple-element.13.w_ref, ...), custom_call_target="tpu_custom_call" | custom-call | tf_op jit(solution)/shard_map/pallas_call | solution.py:488

commit v5 on v4

--- a/solution.py
+++ b/solution.py
@@ -12,7 +12,7 @@
 MESH = pl.DeviceIdType.MESH
 GROUP = 128
 CHUNKS = 4
-ROUNDS = 2
+ROUNDS = 4
 
 
 def halves(wide):
@@ -268,12 +268,16 @@
             device_id_type=MESH,
         )
 
-    def state_copy(slot, send_sem, to_head):
+    rounds = state_in.shape[0]
+    tall = width // rounds
+
+    def state_copy(slot, turn, send_sem, to_head):
+        view = states.at[slot, pl.ds(turn * tall, tall), :]
         return pltpu.make_async_remote_copy(
-            src_ref=states.at[slot],
-            dst_ref=states.at[slot],
+            src_ref=view,
+            dst_ref=view,
             send_sem=send_sem,
-            recv_sem=state_recv.at[slot],
+            recv_sem=state_recv.at[turn, slot],
             device_id=(ctx, to_head),
             device_id_type=MESH,
         )
@@ -309,9 +313,8 @@
     joined = after(second, first)
     joined_map = joined[:, :width]
     joined_add = joined[:, width:].T
-
-    rounds = state_in.shape[0]
-    tall = width // rounds
+    first_map = first[:, :width]
+    first_add = first[:, width:].T
 
     def relay(turn):
         return pltpu.make_async_remote_copy(
@@ -343,17 +346,17 @@
         def _():
             relay(turn).start()
 
-    start = state_in[...].reshape(width, width)
-    states[head] = jnp.where(
-        side == 0, start, dot_rows_wide(start, first[:, :width]) + first[:, width:].T
-    )
-    for step in range(1, chips):
-        copy = state_copy(head, state_send.at[step], chip_at(step) * 2 + core)
+        start = state_in[turn]
+        states[head, rows, :] = jnp.where(
+            side == 0, start, dot_rows_wide(start, first_map) + first_add[rows, :]
+        )
+        for step in range(1, chips):
+            copy = state_copy(head, turn, state_send.at[turn, step], chip_at(step) * 2 + core)
+            copy.start()
+            sent.append(copy)
+        copy = state_copy(head, turn, state_send.at[turn, 0], twin)
         copy.start()
         sent.append(copy)
-    copy = state_copy(head, state_send.at[0], twin)
-    copy.start()
-    sent.append(copy)
 
     def pass_on(chunk):
         for step in range(1, chips):
@@ -373,7 +376,8 @@
     own_start = beside(*halves(states[head]))
     for chunk in range(chunks):
         mine[core, chunk] = settled(parts, head, chunk, own_start, gain, share)
-    state_copy(twin, state_send.at[0], twin).wait_recv()
+    for turn in range(rounds):
+        state_copy(twin, turn, state_send.at[turn, 0], twin).wait_recv()
     twin_start = beside(*halves(states[twin]))
     for chunk in range(chunks):
         part_copy(twin, chunk, part_send.at[chunk, 0], twin).wait_recv()
@@ -383,20 +387,22 @@
     for chunk in range(chunks):
         done[chunk] = dot(beside(mine[0, chunk], mine[1, chunk]), own_weights)
 
-    for step in range(1, chips):
-        slot = chip_at(step) * 2 + core
-        copy = state_copy(slot, state_pass.at[step], twin)
-        copy.wait_recv()
-        copy.start()
-        sent.append(copy)
+    for turn in range(rounds):
+        for step in range(1, chips):
+            slot = chip_at(step) * 2 + core
+            copy = state_copy(slot, turn, state_pass.at[turn, step], twin)
+            copy.wait_recv()
+            copy.start()
+            sent.append(copy)
 
     for chunk in range(chunks):
         for step in range(1, chips):
             slot = chip_at(step) * 2 + 1 - core
             part_copy(slot, chunk, part_pass.at[chunk, step], twin).wait_recv()
-    for step in range(1, chips):
-        slot = chip_at(step) * 2 + 1 - core
-        state_copy(slot, state_pass.at[step], twin).wait_recv()
+    for turn in range(rounds):
+        for step in range(1, chips):
+            slot = chip_at(step) * 2 + 1 - core
+            state_copy(slot, turn, state_pass.at[turn, step], twin).wait_recv()
 
     for copy in sent:
         copy.wait_send()
@@ -474,9 +480,9 @@
                 pltpu.SemaphoreType.DMA((CHUNKS, heads // 2)),
                 pltpu.SemaphoreType.DMA((CHUNKS, heads // 2)),
                 pltpu.SemaphoreType.DMA((CHUNKS, heads)),
-                pltpu.SemaphoreType.DMA((heads // 2,)),
-                pltpu.SemaphoreType.DMA((heads // 2,)),
-                pltpu.SemaphoreType.DMA((heads,)),
+                pltpu.SemaphoreType.DMA((ROUNDS, heads // 2)),
+                pltpu.SemaphoreType.DMA((ROUNDS, heads // 2)),
+                pltpu.SemaphoreType.DMA((ROUNDS, heads)),
             ],
             compiler_params=pltpu.CompilerParams(
                 collective_id=0, has_side_effects=True, vmem_limit_bytes=24 << 20

time: 29.4 us -> 29.4 us (level); the launches traced: 29.3 us -> 29 us
  Pallas kernels: 29.3 us -> 29 us
    pallas_call x1, Pallas kernels: 26.6 us -> 26.3 us  [shards(): pl.pallas_call(functools.partial(kernel, count, heads), out_shape=(jax.Sh...]
where the time goes in v5:
time: 29.4 us; the launch traced here: 29 us
  Pallas kernels  29 us (99%)
    pallas_call x1, Pallas kernels, shards(): pl.pallas_call(functools.partial(kernel, count, heads), out_shape=(jax.Sh...  26.3 us
    pallas_call x1, Pallas kernels, shards(): pl.pallas_call(finish, out_shape=jax.ShapeDtypeStruct((length, columns),...  2.69 us

profile of v5, /device:TPU:25, one launch (start us, length us, event | category | flops | bytes accessed | tf_op | source)
XLA Modules:
  0.0 29.0 jit_solution(1243035043813766811)
XLA Ops:
  0.0 26.3 %shard_map.64 = (bf16[4,4,2,256,128]{4,3,2,1,0:T(8,128)(2,1)S(1)}, f32[4,128,128]{2,1,0:T(8,128)S(1)}, f32[1,128]{1,0:T(1,128)S(1)}, bf16[512,512]{1,0:T(8,128)(2,1)S(1)}, f32[4,256,512]{2,1,0:T(8,128)S(1)}) custom-call(bf16[1024,128]{1,0:T(8,128)(2,1)} %q_hbm.1, bf16[1024,128]{1,0:T(8,128)(2,1)} %k_hbm.1, bf16[1024,128]{1,0:T(8,128)(2,1)} %v_hbm.1, ...), custom_call_target="tpu_custom_call" | custom-call | tf_op jit(solution)/shard_map/pallas_call | solution.py:451
  26.3 2.7 %shard_map.65 = bf16[1024,512]{1,0:T(8,128)(2,1)} custom-call(bf16[4,4,2,256,128]{4,3,2,1,0:T(8,128)(2,1)S(1)} %get-tuple-element.10.parts, f32[4,128,128]{2,1,0:T(8,128)S(1)} %get-tuple-element.11.states, f32[1,128]{1,0:T(1,128)S(1)} %get-tuple-element.12.gain_ref, bf16[512,512]{1,0:T(8,128)(2,1)S(1)} %get-tuple-element.13.w_ref, ...), custom_call_target="tpu_custom_call" | custom-call | tf_op jit(solution)/shard_map/pallas_call | solution.py:494
